TPU v7x, 32 devices: a whole 2x2x4 slice. The times are simulated.
32 devices in a mesh: feat: 8 (over z, y), ex: 4 (over x, core).
Axes of the slice: x: 2, y: 2, z: 4, core: 2. Of those that a mesh axis runs over, the one named last changes fastest.
Arguments:
- examples: bfloat16 [4096, 262144], P('ex', 'feat'), may hold values from -6 to 6
- weights: bfloat16 [262144], P('feat'), may hold values from -0.01171875 to 0.01171875
- labels: int32 [4096], P('ex'), may hold values from 0 to 1
- split: int32 [4096], P('ex'), may hold values 0 or 1
- val_weight: float32 [32, 4096], P(None, 'ex'), may hold values from 0.1 to 10
- strengths: float32 [256], replicated, may hold values from 0.05 to 1
- block_ids: int32 [262144], P('feat'), may hold values from 0 to 255
Outputs:
- solve: float32 [32, 262144], P(None, ('feat', 'ex'))
- hypergrad: float32 [32, 256], P(None, ('feat', 'ex'))
All inputs are finite; a program needn't handle non-finite values. No bound on the sum of `split` on one device may be relied on, other than what follows from the above.
Results may differ from a plain program's by a relative error of at most 0.0029.
Values may be sent and summed in bfloat16 or wider, within the bound.
A program may use at most 128 MiB of HBM per device.

v0:
```python
import functools

import jax
import jax.numpy as jnp
from jax import lax
from jax.experimental import pallas as pl
from jax.experimental.pallas import tpu as pltpu
from jax.sharding import PartitionSpec as P

MESH = pl.DeviceIdType.MESH
VMEM = pl.BlockSpec(memory_space=pltpu.VMEM)
LANES = 128


def address(axis, pos):
    if axis == "feat":
        return (pos, lax.axis_index("ex"))
    return (lax.axis_index("feat"), pos)


def flip(pos, offset):
    out, mask = pos, 1
    while mask <= offset:
        if offset & mask:
            out = out + mask * (1 - 2 * lax.rem(lax.div(pos, mask), 2))
        mask *= 2
    return out


def meet(axis, peers):
    barrier = pltpu.get_barrier_semaphore()
    for peer in peers:
        pl.semaphore_signal(barrier, inc=1, device_id=address(axis, peer), device_id_type=MESH)
    pl.semaphore_wait(barrier, len(peers))


def total_kernel(axis, n, x_ref, out_ref, slots, send_sem, recv_sem):
    me = lax.axis_index(axis)
    peers = [lax.rem(me + k, n) for k in range(1, n)]
    meet(axis, peers)
    copies = []
    for k, peer in enumerate(peers):
        copy = pltpu.make_async_remote_copy(
            src_ref=x_ref,
            dst_ref=slots.at[k],
            send_sem=send_sem.at[k],
            recv_sem=recv_sem.at[k],
            device_id=address(axis, peer),
            device_id_type=MESH,
        )
        copy.start()
        copies.append(copy)
    total = x_ref[...]
    for k, copy in enumerate(copies):
        copy.wait_recv()
        total = total + slots[k]
    out_ref[...] = total
    for copy in copies:
        copy.wait_send()


def small_total(x, axis, ident):
    n = lax.axis_size(axis)
    if n == 1:
        return x
    return pl.pallas_call(
        functools.partial(total_kernel, axis, n),
        out_shape=jax.ShapeDtypeStruct(x.shape, x.dtype),
        in_specs=[VMEM],
        out_specs=VMEM,
        scratch_shapes=[
            pltpu.VMEM((n - 1,) + x.shape, x.dtype),
            pltpu.SemaphoreType.DMA((n - 1,)),
            pltpu.SemaphoreType.DMA((n - 1,)),
        ],
        compiler_params=pltpu.CompilerParams(collective_id=ident, has_side_effects=True),
    )(x)


def reduce_kernel(axis, n, x_ref, out_ref, slots, full, send_sem, recv_sem):
    me = lax.axis_index(axis)
    peers = [lax.rem(me + k, n) for k in range(1, n)]
    meet(axis, peers)
    first, second = [], []
    for k, peer in enumerate(peers):
        copy = pltpu.make_async_remote_copy(
            src_ref=x_ref.at[peer],
            dst_ref=slots.at[k],
            send_sem=send_sem.at[0, k],
            recv_sem=recv_sem.at[0, k],
            device_id=address(axis, peer),
            device_id_type=MESH,
        )
        copy.start()
        first.append(copy)
    total = x_ref[me]
    for k, copy in enumerate(first):
        copy.wait_recv()
        total = total + slots[k]
    full[me] = total
    for k, peer in enumerate(peers):
        copy = pltpu.make_async_remote_copy(
            src_ref=full.at[me],
            dst_ref=full.at[me],
            send_sem=send_sem.at[1, k],
            recv_sem=recv_sem.at[1, k],
            device_id=address(axis, peer),
            device_id_type=MESH,
        )
        copy.start()
        second.append(copy)
    for copy in second:
        copy.wait_recv()
    out_ref[...] = full[...]
    for copy in first + second:
        copy.wait_send()


def large_total(x, axis, ident):
    n = lax.axis_size(axis)
    if n == 1:
        return x
    rows = x.shape[0]
    y = x.reshape(n, rows // n, LANES)
    out = pl.pallas_call(
        functools.partial(reduce_kernel, axis, n),
        out_shape=jax.ShapeDtypeStruct(y.shape, y.dtype),
        in_specs=[VMEM],
        out_specs=VMEM,
        scratch_shapes=[
            pltpu.VMEM((n - 1,) + y.shape[1:], y.dtype),
            pltpu.VMEM(y.shape, y.dtype),
            pltpu.SemaphoreType.DMA((2, n - 1)),
            pltpu.SemaphoreType.DMA((2, n - 1)),
        ],
        compiler_params=pltpu.CompilerParams(collective_id=ident, has_side_effects=True),
    )(y)
    return out.reshape(rows, LANES)


def spread_kernel(n, share, pieces, based, *refs):
    if based:
        x_ref, base_ref, coef_ref, own_ref, all_ref = refs[:5]
    else:
        x_ref, own_ref, all_ref = refs[:3]
    scratch = refs[-8:]
    me = lax.axis_index("ex")
    masks = []
    while 2 ** len(masks) < n:
        masks.append(2 ** len(masks))
    meet("ex", [flip(me, mask) for mask in masks])
    if based:
        ends = (base_ref, coef_ref, own_ref, all_ref)
    else:
        ends = (None, None, own_ref, all_ref)
    lanes = [
        spread_piece(n, share, share // pieces, piece, masks, x_ref, ends, *[r.at[piece] for r in scratch])
        for piece in range(pieces)
    ]
    while lanes:
        lanes = [lane for lane in lanes if next(lane, None)]


def spread_piece(n, share, size, piece, masks, x_ref, ends, acc, outbox, inbox, full, out_sem, in_sem, send_sem, recv_sem):
    base_ref, coef_ref, own_ref, all_ref = ends
    me = lax.axis_index("ex")

    def columns(chunk):
        return pl.ds(pl.multiple_of(chunk * share + piece * size, LANES), size)

    here = pl.ds(piece * size, size)
    copies = []
    slot = 0
    for level, mask in enumerate(masks):
        low = lax.rem(me, mask)
        bit = lax.rem(lax.div(me, mask), 2)
        groups = n // (2 * mask)
        upper = lax.div(me, 2 * mask)
        sent = []
        for k in range(groups):
            group = lax.rem(upper + 1 + k, groups) if groups > 1 else 0
            away = group * 2 * mask + (1 - bit) * mask + low
            kept = group * 2 * mask + bit * mask + low
            if level == 0:
                part = x_ref[:, columns(away)]
            else:
                part = acc[away]
            outbox[slot] = part.astype(jnp.bfloat16)
            copy = pltpu.make_async_remote_copy(
                src_ref=outbox.at[slot],
                dst_ref=inbox.at[slot],
                send_sem=out_sem.at[slot],
                recv_sem=in_sem.at[slot],
                device_id=address("ex", flip(me, mask)),
                device_id_type=MESH,
            )
            copy.start()
            sent.append((copy, kept, slot))
            slot += 1
        yield True
        nexts = []
        for copy, kept, at in sent:
            if level == 0:
                mine = x_ref[:, columns(kept)]
            else:
                mine = acc[kept]
            nexts.append((copy, kept, at, mine))
        for copy, kept, at, mine in nexts:
            copy.wait_recv()
            acc[kept] = mine + inbox[at].astype(jnp.float32)
            copies.append(copy)
    own = acc[me] if n > 1 else x_ref[:, here]
    if base_ref is not None:
        own = base_ref[:, here] + coef_ref[:, 0:1] * own
    own_ref[:, here] = own
    full[me] = own.astype(jnp.bfloat16)

    ident = {}
    held = [0]
    order = []
    for mask in reversed(masks):
        for offset in held:
            ident[mask, offset] = len(ident)
        order.append((mask, list(held)))
        held = held + [mask ^ offset for offset in held]

    def passing(mask, offset):
        at = ident[mask, offset]
        chunk = flip(me, offset)
        return pltpu.make_async_remote_copy(
            src_ref=full.at[chunk],
            dst_ref=full.at[chunk],
            send_sem=send_sem.at[at],
            recv_sem=recv_sem.at[at],
            device_id=address("ex", flip(me, mask)),
            device_id_type=MESH,
        )

    live = {}
    for mask in reversed(masks):
        live[mask, 0] = passing(mask, 0)
        live[mask, 0].start()
    all_ref[:, columns(me)] = full[me]
    for mask, offsets in order:
        yield True
        for offset in offsets:
            live[mask, offset].wait_recv()
            arrived = mask ^ offset
            for smaller in reversed(masks):
                if smaller < mask:
                    live[smaller, arrived] = passing(smaller, arrived)
                    live[smaller, arrived].start()
            chunk = flip(me, arrived)
            all_ref[:, columns(chunk)] = full[chunk]
    yield True
    for copy in copies:
        copy.wait_send()
    for copy in live.values():
        copy.wait_send()


def spread(x, base, coef, ident):
    n = lax.axis_size("ex")
    rows, width = x.shape
    share = width // n
    based = base is not None
    count = max(n - 1, 1)
    pieces = 4 if share % (4 * LANES) == 0 else 1
    size = share // pieces
    return pl.pallas_call(
        functools.partial(spread_kernel, n, share, pieces, based),
        out_shape=(
            jax.ShapeDtypeStruct((rows, share), jnp.float32),
            jax.ShapeDtypeStruct((rows, width), jnp.bfloat16),
        ),
        in_specs=[VMEM] * (3 if based else 1),
        out_specs=(VMEM, VMEM),
        scratch_shapes=[
            pltpu.VMEM((pieces, n, rows, size), jnp.float32),
            pltpu.VMEM((pieces, count, rows, size), jnp.bfloat16),
            pltpu.VMEM((pieces, count, rows, size), jnp.bfloat16),
            pltpu.VMEM((pieces, n, rows, size), jnp.bfloat16),
        ]
        + [pltpu.SemaphoreType.DMA((pieces, count))] * 4,
        compiler_params=pltpu.CompilerParams(collective_id=ident, has_side_effects=True),
    )(*((x, base, coef) if based else (x,)))


def to_rows(x):
    rows, cols = x.shape
    if cols % LANES == 0:
        return x.reshape(rows, cols // LANES, LANES).transpose(1, 0, 2).reshape(-1, LANES)
    flat = x.reshape(-1)
    return jnp.pad(flat, (0, -flat.shape[0] % LANES)).reshape(-1, LANES)


def from_rows(x, shape):
    rows, cols = shape
    if cols % LANES == 0:
        return x.reshape(cols // LANES, rows, LANES).transpose(1, 0, 2).reshape(rows, cols)
    return x.reshape(-1)[: rows * cols].reshape(rows, cols)


def pack(arrays, multiple):
    out = jnp.concatenate([to_rows(x) for x in arrays], axis=0)
    return jnp.pad(out, ((0, -out.shape[0] % multiple), (0, 0)))


def unpack(x, arrays):
    out, at = [], 0
    for like in arrays:
        count = -(-like.shape[0] * like.shape[1] // LANES)
        out.append(from_rows(x[at : at + count], like.shape))
        at += count
    return out


def shards(examples, weights, labels, split, val_weight, strengths, block_ids):
    n_ex = lax.axis_size("ex")
    n_feat = lax.axis_size("feat")
    ex_pos = lax.axis_index("ex")
    feat_pos = lax.axis_index("feat")
    total = examples.shape[0] * n_ex
    width = examples.shape[1]
    share = width // n_ex
    blocks = strengths.shape[0]
    nb_feat = blocks // n_feat
    nb_local = nb_feat // n_ex
    start = ex_pos * share

    def reduced(x, pieces):
        parts = []
        for _ in range(pieces):
            part = lax.reduce_precision(x, 8, 7)
            parts.append(part.astype(jnp.bfloat16))
            x = x - part
        return parts

    part = jnp.dot(examples, weights, preferred_element_type=jnp.float32)
    (margin,) = unpack(small_total(pack([part[None, :]], 8), "feat", 0), [part[None, :]])
    margin = margin[0]
    prob = 1.0 / (1.0 + jnp.exp(-margin))
    train = split.astype(jnp.float32)
    curvew = train * prob * (1.0 - prob)
    err = (1.0 - train) * (prob - labels.astype(jnp.float32))
    gradw = (val_weight * err[None, :] / jnp.sqrt(jnp.float32(total))).astype(jnp.bfloat16)
    rhs, low = spread(jnp.dot(gradw, examples, preferred_element_type=jnp.float32), None, None, 1)

    ids_loc = lax.dynamic_slice_in_dim(block_ids, start, share, 0)
    w_loc = lax.dynamic_slice_in_dim(weights, start, share, 0).astype(jnp.float32)
    onehot = (ids_loc[:, None] == jnp.arange(blocks, dtype=jnp.int32)[None, :]).astype(jnp.bfloat16)
    levels = jnp.stack(reduced(strengths, 3), axis=0)
    lam = jnp.sum(
        lax.dot_general(levels, onehot, (((1,), (1,)), ((), ())), preferred_element_type=jnp.float32),
        axis=0,
    )

    def tangents(direc):
        return lax.dot_general(
            direc, examples, (((1,), (1,)), ((), ())), preferred_element_type=jnp.float32
        )

    scaled = lam[None, :] * rhs
    sums = jnp.stack([jnp.sum(rhs * rhs, axis=1), jnp.sum(scaled * rhs, axis=1)])
    part = tangents(low)
    tang, sums = unpack(large_total(pack([part, sums], 8 * n_feat), "feat", 2), [part, sums])
    weighted = curvew[None, :] * tang
    sums = jnp.concatenate([sums, jnp.sum(weighted * tang, axis=1)[None, :]])
    (sums,) = unpack(small_total(pack([sums], 8), "ex", 3), [sums])
    norm_now, damp, along = sums[0], sums[1], sums[2]
    alpha = norm_now / (along / jnp.float32(total) + damp)

    prod = jnp.dot(weighted.astype(jnp.bfloat16), examples, preferred_element_type=jnp.float32)
    coef = jnp.broadcast_to((-alpha / jnp.float32(total))[:, None], (alpha.shape[0], LANES))
    resid, low = spread(prod, rhs - alpha[:, None] * scaled, coef, 4)

    stepped = lam[None, :] * resid
    sums = jnp.stack(
        [
            jnp.sum(resid * resid, axis=1),
            jnp.sum(stepped * resid, axis=1),
            jnp.sum(stepped * rhs, axis=1),
        ]
    )
    both = jnp.concatenate([rhs, resid]) * w_loc[None, :]
    pieces = jnp.concatenate(reduced(both, 2))
    rows = both.shape[0]
    grouped = jnp.dot(pieces, onehot, preferred_element_type=jnp.float32)
    grouped = grouped[:rows] + grouped[rows:]
    part = tangents(low)
    parts = [part, grouped, sums]
    turned, grouped, sums = unpack(large_total(pack(parts, 8 * n_feat), "feat", 5), parts)
    grouped = lax.dynamic_slice_in_dim(grouped, feat_pos * nb_feat, nb_feat, 1)
    heavy = curvew[None, :] * turned
    sums = jnp.concatenate(
        [sums, jnp.sum(heavy * turned, axis=1)[None, :], jnp.sum(heavy * tang, axis=1)[None, :]]
    )
    parts = [grouped, sums]
    grouped, sums = unpack(small_total(pack(parts, 8), "ex", 6), parts)
    norm_next = sums[0]
    beta = norm_next / norm_now
    curved = sums[3] + 2.0 * beta * sums[4] + beta * beta * along
    damped = sums[1] + 2.0 * beta * sums[2] + beta * beta * damp
    step = norm_next / (curved / jnp.float32(total) + damped)
    first = alpha + step * beta
    solve = first[:, None] * rhs + step[:, None] * resid
    grouped = lax.dynamic_slice_in_dim(grouped, ex_pos * nb_local, nb_local, 1)
    half = rows // 2
    block_sums = first[:, None] * grouped[:half] + step[:, None] * grouped[half:]
    own = lax.dynamic_slice_in_dim(
        strengths, (feat_pos * n_ex + ex_pos) * nb_local, nb_local, 0
    )
    return (solve, -own[None, :] * block_sums)


def solution(mesh):
    placed = (P("ex", "feat"), P("feat"), P("ex"), P("ex"), P(None, "ex"), P(), P("feat"))
    return jax.shard_map(
        shards,
        mesh=mesh,
        in_specs=placed,
        out_specs=(P(None, ("feat", "ex")), P(None, ("feat", "ex"))),
        check_vma=False,
    )
```

profile of v0, /device:TPU:0, one launch (start us, length us, event | category | flops | bytes accessed | tf_op | source)
XLA Modules:
  0.0 280.6 jit_solution(150778482704988172)
XLA Ops:
  0.6 0.8 dynamic_slice.15
  1.4 0.7 reduce-precision_convert_fusion.2
  2.1 2.1 fusion.10
  4.2 0.9 reshape.196
  5.2 27.3 %fusion.46 = f32[1,1024]{1,0:T(1,128)} fusion(bf16[1024,32768]{1,0:T(8,128)(2,1)} %param.7, bf16[32768,1]{0,1:T(2,128)(2,1)S(1)} %reshape.196), kind=kOutput, calls=%fused_computation.101 | convolution fusion | flops 67108864 | bytes 67178496 | tf_op jit(solution)/shard_map/dot_general | solution.py:339
  32.4 9.7 %shard_map.86 = f32[8,128]{1,0:T(8,128)} custom-call(f32[8,128]{1,0:T(8,128)} %bitcast.133), custom_call_target="tpu_custom_call" | custom-call | tf_op jit(solution)/shard_map/pallas_call | solution.py:66
  42.2 0.7 fusion.27
  42.9 25.3 %fusion.18.refs_0_ = f32[32,32768]{1,0:T(8,128)} fusion(bf16[1024,32768]{1,0:T(8,128)(2,1)} %param.7, f32[32,1024]{1,0:T(8,128)S(1)} %copy-done.2, f32[1024]{0:T(1024)S(1)} %get-tuple-element.28), kind=kOutput, calls=%fused_computation.41 | convolution fusion | flops 2147581952 | bytes 71438336 | tf_op jit(solution)/shard_map/dot_general | solution.py:347
  68.2 32.2 %shard_map.87 = (f32[32,8192]{1,0:T(8,128)}, bf16[32,32768]{1,0:T(8,128)(2,1)}) custom-call(f32[32,32768]{1,0:T(8,128)} %fusion.18.refs_0_), custom_call_target="tpu_custom_call" | custom-call | tf_op jit(solution)/shard_map/pallas_call | solution.py:270
  100.4 1.5 multiply_reduce_fusion.1
  101.9 0.1 reshape.171
  102.0 29.1 %convolution_bitcast_fusion.1 = f32[4,8,8,128]{3,1,2,0:T(8,128)S(1)} fusion(bf16[32,32768]{1,0:T(8,128)(2,1)} %get-tuple-element.6, bf16[1024,32768]{1,0:T(8,128)(2,1)} %param.7), kind=kOutput, calls=%fused_computation.19 | convolution fusion | flops 2147483648 | bytes 69337088 | tf_op jit(solution)/shard_map/dot_general | solution.py:359
  131.2 0.7 select_maximum_fusion.2
  131.9 16.2 %shard_map.88 = f32[8,40,128]{2,1,0:T(8,128)} custom-call(f32[8,40,128]{2,1,0:T(8,128)} %bitcast.119), custom_call_target="tpu_custom_call" | custom-call | tf_op jit(solution)/shard_map/pallas_call | solution.py:125
  148.1 0.9 slice.104
  149.0 0.1 fusion.16
  149.1 0.7 slice_reduce_fusion.1
  149.8 0.1 reshape.175
  149.9 0.1 reshape.177
  150.0 0.6 pad.34.x_ref
  150.6 4.9 %shard_map.89 = f32[8,128]{1,0:T(8,128)} custom-call(f32[8,128]{1,0:T(8,128)} %pad.34.x_ref), custom_call_target="tpu_custom_call" | custom-call | tf_op jit(solution)/shard_map/pallas_call | solution.py:66
  155.6 0.9 negate_multiply_fusion
  156.4 1.2 fusion.9.refs_1_
  157.6 0.7 broadcast_in_dim.9.refs_2_
  158.3 25.3 %fusion.19.refs_0_ = f32[32,32768]{1,0:T(8,128)} fusion(bf16[1024,32768]{1,0:T(8,128)(2,1)} %param.7, f32[8,4,8,128]{3,2,1,0:T(8,128)S(1)} %bitcast.113, f32[1024]{0:T(1024)S(1)} %get-tuple-element.27), kind=kOutput, calls=%fused_computation.42 | convolution fusion | flops 2147549184 | bytes 71438336 | tf_op jit(solution)/shard_map/dot_general | solution.py:373
  183.5 32.5 %shard_map.90 = (f32[32,8192]{1,0:T(8,128)}, bf16[32,32768]{1,0:T(8,128)(2,1)}) custom-call(f32[32,32768]{1,0:T(8,128)} %fusion.19.refs_0_, f32[32,8192]{1,0:T(8,128)} %fusion.9.refs_1_, f32[32,128]{1,0:T(8,128)} %broadcast_in_dim.9.refs_2_), custom_call_target="tpu_custom_call" | custom-call | tf_op jit(solution)/shard_map/pallas_call | solution.py:270
  216.1 0.7 dynamic-slice_convert_fusion
  216.8 1.6 reduce-precision_convert_fusion
  218.4 1.6 fusion
  220.1 29.1 %convolution_bitcast_fusion = f32[4,8,8,128]{3,1,2,0:T(8,128)S(1)} fusion(bf16[32,32768]{1,0:T(8,128)(2,1)} %get-tuple-element.8, bf16[1024,32768]{1,0:T(8,128)(2,1)} %param.7), kind=kOutput, calls=%fused_computation.18 | convolution fusion | flops 2147483648 | bytes 69337088 | tf_op jit(solution)/shard_map/dot_general | solution.py:359
  249.4 0.4 fusion.12
  249.8 0.1 reshape.184
  249.9 0.7 select_maximum_fusion
  250.6 16.9 %shard_map.91 = f32[8,56,128]{2,1,0:T(8,128)} custom-call(f32[8,56,128]{2,1,0:T(8,128)} %bitcast.115), custom_call_target="tpu_custom_call" | custom-call | tf_op jit(solution)/shard_map/pallas_call | solution.py:125
  267.6 0.8 slice.107
  268.4 0.1 constant_dynamic-slice_fusion
  268.6 0.9 slice.109
  269.5 0.1 fusion.14
  269.6 0.7 slice_reduce_fusion
  270.3 0.1 reshape.191
  270.5 0.6 select_maximum_fusion.3.x_ref
  271.1 5.1 %shard_map.92 = f32[24,128]{1,0:T(8,128)} custom-call(f32[24,128]{1,0:T(8,128)} %select_maximum_fusion.3.x_ref), custom_call_target="tpu_custom_call" | custom-call | tf_op jit(solution)/shard_map/pallas_call | solution.py:66
  276.2 0.7 slice.100
  277.0 0.7 slice_bitcast_fusion
  277.6 0.9 multiply_add_fusion.1
  278.6 0.1 fusion.25
  278.7 0.7 copy.25
  279.3 1.2 multiply_add_fusion
  (35 shorter events, 0.6 us)
Async XLA Ops:
  5.1 37.1 %copy-start.3 = (s32[1024]{0:T(1024)S(1)}, s32[1024]{0:T(1024)}, u32[]{:S(2)}) copy-start(s32[1024]{0:T(1024)} %param.10) | copy-start | bytes 12292
  5.1 37.1 %copy-start.4 = (s32[1024]{0:T(1024)S(1)}, s32[1024]{0:T(1024)}, u32[]{:S(2)}) copy-start(s32[1024]{0:T(1024)} %param.9) | copy-start | bytes 12292
  5.2 37.8 %copy-start.2 = (f32[32,1024]{1,0:T(8,128)S(1)}, f32[32,1024]{1,0:T(8,128)}, u32[]{:S(2)}) copy-start(f32[32,1024]{1,0:T(8,128)} %param.11) | copy-start | bytes 393220
  102.0 54.4 %copy-start = (f32[32,8192]{1,0:T(8,128)S(1)}, f32[32,8192]{1,0:T(8,128)}, u32[]{:S(2)}) copy-start(f32[32,8192]{1,0:T(8,128)} %get-tuple-element.7) | copy-start | bytes 3145732
  220.1 29.2 %copy-start.1 = (f32[32,8192]{1,0:T(8,128)S(1)}, f32[32,8192]{1,0:T(8,128)}, u32[]{:S(2)}) copy-start(f32[32,8192]{1,0:T(8,128)} %get-tuple-element.9) | copy-start | bytes 3145732
  249.3 29.2 %copy-start.5 = (f32[256]{0:T(256)S(1)}, f32[256]{0:T(256)}, u32[]{:S(2)}) copy-start(f32[256]{0:T(256)} %param.12) | copy-start | bytes 3076
where the time goes:
time: 282 us; the launch traced here: 281 us
  matrix products  140 us (50%)
  Pallas kernels  118 us (42%)
  other arithmetic  12.2 us (4%)
  local copies, waits for them, and re-layouts  10 us (4%)
    pallas_call x2, Pallas kernels, spread(): pl.pallas_call(functools.partial(spread_kernel, n, share, pieces, based),...  64.8 us
    dot_general x2, matrix products, tangents(): lax.dot_general(direc, examples, (((1,), (1,)), ((), ())), preferred_elem...  58.2 us
    pallas_call x2, Pallas kernels, large_total(): pl.pallas_call(functools.partial(reduce_kernel, axis, n), out_shape=jax.S...  33.1 us
    dot_general x1, matrix products, shards(): part = jnp.dot(examples, weights, preferred_element_type=jnp.float32)  27.3 us
    dot_general x1, matrix products, shards(): jnp.dot(gradw, examples, preferred_element_type=jnp.float32)  25.3 us
    dot_general x1, matrix products, shards(): jnp.dot(weighted.astype(jnp.bfloat16), examples, preferred_element_type=j...  25.3 us
    pallas_call x3, Pallas kernels, small_total(): pl.pallas_call(functools.partial(total_kernel, axis, n), out_shape=jax.Sh...  19.7 us

commit v1 on v0

v1 whole, which is shorter than its diff:
```python
import functools
import math

import jax
import jax.numpy as jnp
from jax import lax
from jax.experimental import pallas as pl
from jax.experimental.pallas import tpu as pltpu
from jax.sharding import PartitionSpec as P

MESH = pl.DeviceIdType.MESH
VMEM = pl.BlockSpec(memory_space=pltpu.VMEM)
ANY = pl.BlockSpec(memory_space=pl.ANY)
LANES = 128
LAG_SUM, LAG_LOW, LAG_TANG = 1, 3, 4
RING_BYTES = 32 * 2**20


def address(axis, pos):
    if axis == "feat":
        return (pos, lax.axis_index("ex"))
    return (lax.axis_index("feat"), pos)


def flip(pos, mask):
    return pos + mask * (1 - 2 * lax.rem(lax.div(pos, mask), 2))


def fold(x):
    total = x[:, :LANES]
    for at in range(LANES, x.shape[1], LANES):
        total = total + x[:, at : at + LANES]
    return total


def pick(packet, lane):
    lanes = lax.broadcasted_iota(jnp.int32, packet.shape, 1)
    return jnp.sum(jnp.where(lanes == lane, packet, 0.0), axis=1, keepdims=True)


def packed(columns, rows):
    lanes = lax.broadcasted_iota(jnp.int32, (rows, LANES), 1)
    out = jnp.zeros((rows, LANES), jnp.float32)
    for lane, column in enumerate(columns):
        out = jnp.where(lanes == lane, column, out)
    return out


def split_in(x, pieces):
    parts = []
    for _ in range(pieces):
        part = x.astype(jnp.bfloat16)
        parts.append(part)
        x = x - part.astype(jnp.float32)
    return parts


def one_hot(ids, blocks):
    rows = lax.broadcasted_iota(jnp.int32, (blocks, ids.shape[1]), 0)
    return (rows == ids).astype(jnp.float32).astype(jnp.bfloat16)


def kernel(
    dims,
    x_hbm,
    w_ref,
    ids_ref,
    labels_ref,
    split_ref,
    vw_ref,
    strengths_ref,
    solve_ref,
    hyper_ref,
    ring,
    margin,
    margins,
    lam,
    curvew,
    left,
    keep,
    out_a,
    in_a,
    out_b,
    in_b,
    low,
    rhs,
    tang,
    parts,
    gathered,
    sums,
    coef,
    packets,
    grouped,
    groups,
    group_parts,
    own_groups,
    own_parts,
    own_strengths,
    ring_sem,
    pair_sem,
    feat_sem,
    ex_sem,
):
    nf, ne, n, width, rows, blocks, share, size, chunks, slots = dims
    total = n * ne
    groups_n = n // LANES
    owners = min(nf, groups_n)
    per = groups_n // owners
    nb_feat = blocks // nf
    nb_own = nb_feat // ne
    me_f = lax.axis_index("feat")
    me_e = lax.axis_index("ex")
    core = lax.rem(me_e, 2)
    side = lax.div(me_e, 2)
    half = 2 * size

    barrier = pltpu.get_barrier_semaphore()
    for axis, me, count in (("feat", me_f, nf), ("ex", me_e, ne)):
        for k in range(1, count):
            pl.semaphore_signal(
                barrier, inc=1, device_id=address(axis, lax.rem(me + k, count)), device_id_type=MESH
            )

    def load(turn):
        chunk = lax.rem(turn, chunks)
        slot = lax.rem(turn, slots)
        copies = []
        for h in range(2):
            for x in range(2):
                at = pl.multiple_of((h + 2 * x) * share + chunk * size, LANES)
                copies.append(
                    pltpu.make_async_copy(
                        x_hbm.at[:, pl.ds(at, size)],
                        ring.at[slot, :, pl.ds(h * half + x * size, size)],
                        ring_sem.at[slot, 2 * h + x],
                    )
                )
        return copies

    def begin(turn):
        for copy in load(turn):
            copy.start()

    def arrived(turn):
        for copy in load(turn):
            copy.wait()

    def refill(turn):
        @pl.when(turn + slots < 3 * chunks)
        def _():
            begin(turn + slots)

    for turn in range(min(slots, 3 * chunks)):
        begin(turn)

    def columns(ref, chunk, h, x):
        at = pl.multiple_of((h + 2 * x) * share + chunk * size, LANES)
        return ref[:, pl.ds(at, size)]

    levels = jnp.concatenate(
        split_in(strengths_ref[...], 3) + [jnp.zeros((5, blocks), jnp.bfloat16)], axis=0
    )
    own_strengths[...] = jnp.transpose(jnp.broadcast_to(strengths_ref[...], (8, blocks)))
    margin[...] = jnp.zeros_like(margin)

    @pl.loop(0, chunks)
    def _(i):
        arrived(i)
        slot = lax.rem(i, slots)
        w = jnp.concatenate([columns(w_ref, i, h, x) for h in range(2) for x in range(2)], axis=1)
        part = lax.dot_general(
            w.astype(jnp.bfloat16), ring[slot], (((1,), (1,)), ((), ())), preferred_element_type=jnp.float32
        )
        for g in range(groups_n):
            margin[g : g + 1, :] += part[:, g * LANES : (g + 1) * LANES]
        refill(i)
        ids = jnp.concatenate([columns(ids_ref, i, core, x) for x in range(2)], axis=1)
        found = jnp.dot(levels, one_hot(ids, blocks), preferred_element_type=jnp.float32)
        lam[i] = found[0:1] + found[1:2] + found[2:3]

    pl.semaphore_wait(barrier, nf - 1 + ne - 1)

    def remote(src, dst, sems, axis, peer):
        return pltpu.make_async_remote_copy(
            src_ref=src,
            dst_ref=dst,
            send_sem=sems[0],
            recv_sem=sems[1],
            device_id=address(axis, peer),
            device_id_type=MESH,
        )

    def feat_copies(src, dst, kind):
        return [
            remote(src(lax.rem(me_f + k, nf)), dst(k), [feat_sem.at[kind, d, k] for d in range(2)], "feat", lax.rem(me_f + k, nf))
            for k in range(1, nf)
        ]

    def ex_copies(src, dst, kind):
        return [
            remote(src(lax.rem(me_e + k, ne)), dst(k), [ex_sem.at[kind, d, k] for d in range(2)], "ex", lax.rem(me_e + k, ne))
            for k in range(1, ne)
        ]

    def launch(copies):
        for copy in copies:
            copy.start()
        return copies

    waiting = []

    def receive(copies):
        for copy in copies:
            copy.wait_recv()
        waiting.extend(copies)

    receive(launch(feat_copies(lambda peer: margin, lambda k: margins.at[k], 0)))
    whole = margin[...]
    for k in range(1, nf):
        whole = whole + margins[k]
    prob = 1.0 / (1.0 + jnp.exp(-whole))
    train = split_ref[...].astype(jnp.float32)
    curvew[...] = train * prob * (1.0 - prob)
    err = (1.0 - train) * (prob - labels_ref[...].astype(jnp.float32))
    root = jnp.float32(math.sqrt(total))
    for g in range(groups_n):
        at = slice(g * LANES, (g + 1) * LANES)
        left[:, at] = (vw_ref[:, at] * err[g : g + 1] / root).astype(jnp.bfloat16)

    def pair_copy(phase, kind, chunk):
        src, dst, mask = (
            (out_a.at[phase, chunk], in_a.at[phase, chunk], 1),
            (out_b.at[phase, chunk], in_b.at[phase, chunk], 2),
            (low.at[phase, chunk, core], low.at[phase, chunk, core], 1),
        )[kind]
        return remote(src, dst, [pair_sem.at[phase, kind, d, chunk] for d in range(2)], "ex", flip(me_e, mask))

    def product(phase, finish):
        tang[phase] = jnp.zeros_like(tang[phase])
        base = (phase + 1) * chunks

        @pl.loop(0, chunks + LAG_TANG)
        def _(i):
            @pl.when((i >= LAG_LOW) & (i < chunks + LAG_LOW))
            def _():
                chunk = i - LAG_LOW
                pair_copy(phase, 1, chunk).wait_recv()
                value = finish(chunk, keep[chunk] + in_b[phase, chunk].astype(jnp.float32))
                low[phase, chunk, core] = value.astype(jnp.bfloat16)
                pair_copy(phase, 2, chunk).start()

            @pl.when((i >= LAG_SUM) & (i < chunks + LAG_SUM))
            def _():
                chunk = i - LAG_SUM
                pair_copy(phase, 0, chunk).wait_recv()
                value = keep[chunk] + in_a[phase, chunk].astype(jnp.float32)
                keep[chunk] = value
                out_b[phase, chunk] = value.astype(jnp.bfloat16)
                pair_copy(phase, 1, chunk).start()

            @pl.when(i < chunks)
            def _():
                arrived(base + i)
                slot = lax.rem(base + i, slots)
                away = ring[slot, :, pl.ds(pl.multiple_of((1 - core) * half, LANES), half)]
                out_a[phase, i] = jnp.dot(left[...], away, preferred_element_type=jnp.float32).astype(jnp.bfloat16)
                pair_copy(phase, 0, i).start()
                mine = ring[slot, :, pl.ds(pl.multiple_of(core * half, LANES), half)]
                keep[i] = jnp.dot(left[...], mine, preferred_element_type=jnp.float32)

            @pl.when(i >= LAG_TANG)
            def _():
                chunk = i - LAG_TANG
                slot = lax.rem(base + chunk, slots)
                pair_copy(phase, 2, chunk).wait_recv()
                direc = jnp.concatenate([low[phase, chunk, 0], low[phase, chunk, 1]], axis=1)
                part = lax.dot_general(
                    direc, ring[slot], (((1,), (1,)), ((), ())), preferred_element_type=jnp.float32
                )
                for g in range(groups_n):
                    tang[phase, g] += part[:, g * LANES : (g + 1) * LANES]
                refill(base + chunk)

    def scattered(phase):
        peers = [lax.rem(me_f + k, nf) for k in range(1, nf)]
        copies = feat_copies(
            lambda peer: tang.at[phase, pl.ds(lax.rem(peer, owners) * per, per)], lambda k: parts.at[phase, k], 1 + phase
        )
        if owners == nf:
            receive(launch(copies))
        else:
            for peer, copy in zip(peers, copies):
                pl.when(peer < owners)(copy.start)

            @pl.when(me_f < owners)
            def _():
                for copy in copies:
                    copy.wait_recv()

            for peer, copy in zip(peers, copies):
                pl.when(peer < owners)(copy.wait_send)
        value = tang[phase, pl.ds(lax.rem(me_f, owners) * per, per)]
        for k in range(1, nf):
            value = value + parts[phase, k]
        if owners == nf:
            return value
        return jnp.where(me_f < owners, value, 0.0)

    def own_part(ref, chunk):
        return ref[chunk, :, pl.ds(pl.multiple_of(side * size, LANES), size)]

    sums[...] = jnp.zeros_like(sums)

    def first_low(chunk, value):
        rhs[chunk] = value
        own = own_part(rhs, chunk)
        square = own * own
        sums[0] += fold(square)
        sums[1] += fold(square * own_part(lam, chunk))
        return value

    product(0, first_low)

    first_row = lax.rem(me_f, owners) * per

    def weighted(value, other):
        out = jnp.zeros((rows, LANES), jnp.float32)
        for t in range(per):
            out = out + curvew[pl.ds(first_row + t, 1), :] * value[t] * other[t]
        return jnp.sum(out, axis=1, keepdims=True)

    mine = scattered(0)
    gathered[me_f, 0:per] = mine
    gathered[me_f, per] = packed(
        [
            jnp.sum(sums[0], axis=1, keepdims=True),
            jnp.sum(sums[1], axis=1, keepdims=True),
            weighted(mine, mine),
        ],
        rows,
    )
    receive(launch(feat_copies(lambda peer: gathered.at[me_f], lambda k: gathered.at[me_f], 3)))
    packet = gathered[0, per]
    for f in range(1, nf):
        packet = packet + gathered[f, per]
    packets[0, 0] = packet
    shared = launch(ex_copies(lambda peer: packets.at[0, 0], lambda k: packets.at[0, k], 0))
    waiting.extend(shared)
    for g in range(groups_n):
        left[:, g * LANES : (g + 1) * LANES] = (curvew[g : g + 1] * gathered[g // per, g % per]).astype(jnp.bfloat16)

    sums[...] = jnp.zeros_like(sums)
    grouped[...] = jnp.zeros_like(grouped)

    def second_low(chunk, value):
        @pl.when(chunk == 0)
        def _():
            for copy in shared:
                copy.wait_recv()
            packet = packets[0, 0]
            for k in range(1, ne):
                packet = packet + packets[0, k]
            norm, damp, along = (pick(packet, lane) for lane in range(3))
            alpha = norm / (along / total + damp)
            for at, column in enumerate((alpha, norm, damp, along)):
                coef[at] = jnp.broadcast_to(column, (rows, LANES))

        base = rhs[chunk]
        value = base - coef[0, :, 0:1] * (value / total + lam[chunk] * base)
        keep[chunk] = value
        own = own_part(keep, chunk)
        before = own_part(rhs, chunk)
        scaled = own_part(lam, chunk) * own
        sums[0] += fold(own * own)
        sums[1] += fold(scaled * own)
        sums[2] += fold(scaled * before)
        solve_ref[:, pl.ds(pl.multiple_of(chunk * size, LANES), size)] = own
        at = pl.multiple_of(me_e * share + chunk * size, LANES)
        w = w_ref[:, pl.ds(at, size)]
        pieces = jnp.concatenate(split_in(before * w, 2) + split_in(own * w, 2), axis=0)
        grouped[...] += lax.dot_general(
            one_hot(ids_ref[:, pl.ds(at, size)], blocks),
            pieces,
            (((1,), (1,)), ((), ())),
            preferred_element_type=jnp.float32,
        )
        return value

    product(1, second_low)

    for f in range(nf):
        groups[f] = grouped[f * nb_feat : (f + 1) * nb_feat, :]
    sent = launch(feat_copies(lambda peer: groups.at[peer], lambda k: group_parts.at[k], 4))
    turned = scattered(1)
    receive(sent)
    owned = groups[me_f]
    for k in range(1, nf):
        owned = owned + group_parts[k]
    for e in range(ne):
        own_groups[e] = owned[e * nb_own : (e + 1) * nb_own, :]
    held = gathered[me_f, 0:per]
    packets[1, 0] = packed(
        [jnp.sum(sums[at], axis=1, keepdims=True) for at in range(3)]
        + [weighted(turned, turned), weighted(turned, held)],
        rows,
    )
    receive(
        launch(
            ex_copies(lambda peer: packets.at[1, 0], lambda k: packets.at[1, k], 1)
            + ex_copies(lambda peer: own_groups.at[peer], lambda k: own_parts.at[k], 2)
        )
    )
    packet = packets[1, 0]
    for k in range(1, ne):
        packet = packet + packets[1, k]
    packets[2, 0] = packet
    receive(launch(feat_copies(lambda peer: packets.at[2, 0], lambda k: parts.at[2, k, 0], 5)))
    for k in range(1, nf):
        packet = packet + parts[2, k, 0]

    norm_next, damp_next, damp_cross, curved_next, curved_cross = (pick(packet, lane) for lane in range(5))
    alpha, norm, damp, along = (coef[at, :, 0:1] for at in range(4))
    beta = norm_next / norm
    curved = curved_next + 2.0 * beta * curved_cross + beta * beta * along
    damped = damp_next + 2.0 * beta * damp_cross + beta * beta * damp
    step = norm_next / (curved / total + damped)
    first = alpha + step * beta

    @pl.loop(0, chunks)
    def _(i):
        at = pl.ds(pl.multiple_of(i * size, LANES), size)
        solve_ref[:, at] = first * own_part(rhs, i) + step * solve_ref[:, at]

    mine = own_groups[me_e]
    for k in range(1, ne):
        mine = mine + own_parts[k]
    first_block = (me_f * ne + me_e) * nb_own
    scale = own_strengths[pl.ds(first_block, nb_own), 0:1]
    mine = jnp.concatenate([-scale * mine, jnp.zeros((8 * pl.cdiv(nb_own, 8) - nb_own, LANES), jnp.float32)], axis=0) if nb_own % 8 else -scale * mine
    mine = jnp.transpose(mine)[:, :nb_own]
    hyper_ref[...] = first * (mine[:rows] + mine[rows : 2 * rows]) + step * (
        mine[2 * rows : 3 * rows] + mine[3 * rows : 4 * rows]
    )

    for copy in waiting:
        copy.wait_send()

    @pl.loop(0, chunks)
    def _(i):
        for phase in range(2):
            for kind in range(3):
                pair_copy(phase, kind, i).wait_send()


def shards(examples, weights, labels, split, val_weight, strengths, block_ids):
    ne = lax.axis_size("ex")
    nf = lax.axis_size("feat")
    n, width = examples.shape
    rows = val_weight.shape[0]
    blocks = strengths.shape[0]
    share = width // ne
    size = LANES
    while size < 512 and share % (2 * size) == 0:
        size *= 2
    chunks = share // size
    slots = max(LAG_TANG + 2, RING_BYTES // (2 * n * ne * size))
    groups_n = n // LANES
    per = groups_n // min(nf, groups_n)
    nb_feat = blocks // nf
    nb_own = nb_feat // ne
    dims = (nf, ne, n, width, rows, blocks, share, size, chunks, slots)
    half = 2 * size
    f32, bf16 = jnp.float32, jnp.bfloat16
    return pl.pallas_call(
        functools.partial(kernel, dims),
        out_shape=(
            jax.ShapeDtypeStruct((rows, share), f32),
            jax.ShapeDtypeStruct((rows, nb_own), f32),
        ),
        in_specs=[ANY] + [VMEM] * 6,
        out_specs=(VMEM, VMEM),
        scratch_shapes=[
            pltpu.VMEM((slots, n, 2 * half), bf16),
            pltpu.VMEM((groups_n, LANES), f32),
            pltpu.VMEM((nf, groups_n, LANES), f32),
            pltpu.VMEM((chunks, 1, half), f32),
            pltpu.VMEM((groups_n, LANES), f32),
            pltpu.VMEM((rows, n), bf16),
            pltpu.VMEM((chunks, rows, half), f32),
            pltpu.VMEM((2, chunks, rows, half), bf16),
            pltpu.VMEM((2, chunks, rows, half), bf16),
            pltpu.VMEM((2, chunks, rows, half), bf16),
            pltpu.VMEM((2, chunks, rows, half), bf16),
            pltpu.VMEM((2, chunks, 2, rows, half), bf16),
            pltpu.VMEM((chunks, rows, half), f32),
            pltpu.VMEM((2, groups_n, rows, LANES), f32),
            pltpu.VMEM((3, nf, per, rows, LANES), f32),
            pltpu.VMEM((nf, per + 1, rows, LANES), f32),
            pltpu.VMEM((3, rows, LANES), f32),
            pltpu.VMEM((4, rows, LANES), f32),
            pltpu.VMEM((3, ne, rows, LANES), f32),
            pltpu.VMEM((blocks, 4 * rows), f32),
            pltpu.VMEM((nf, nb_feat, 4 * rows), f32),
            pltpu.VMEM((nf, nb_feat, 4 * rows), f32),
            pltpu.VMEM((ne, nb_own, 4 * rows), f32),
            pltpu.VMEM((ne, nb_own, 4 * rows), f32),
            pltpu.VMEM((blocks, 8), f32),
            pltpu.SemaphoreType.DMA((slots, 4)),
            pltpu.SemaphoreType.DMA((2, 3, 2, chunks)),
            pltpu.SemaphoreType.DMA((6, 2, nf)),
            pltpu.SemaphoreType.DMA((3, 2, ne)),
        ],
        compiler_params=pltpu.CompilerParams(
            collective_id=0, has_side_effects=True, vmem_limit_bytes=60 * 2**20
        ),
    )(
        examples,
        weights.astype(f32).reshape(1, width),
        block_ids.reshape(1, width),
        labels.reshape(groups_n, LANES),
        split.reshape(groups_n, LANES),
        val_weight,
        strengths.reshape(1, blocks),
    )


def solution(mesh):
    placed = (P("ex", "feat"), P("feat"), P("ex"), P("ex"), P(None, "ex"), P(), P("feat"))
    return jax.shard_map(
        shards,
        mesh=mesh,
        in_specs=placed,
        out_specs=(P(None, ("feat", "ex")), P(None, ("feat", "ex"))),
        check_vma=False,
    )
```

time: 282 us -> 156 us (0.55)
  matrix products: 140 us -> 0 us
  Pallas kernels: 118 us -> 150 us
  other arithmetic: 12.2 us -> 1.5 us
  local copies, waits for them, and re-layouts: 10 us -> 3.64 us
    dot_general x7 -> x0, matrix products: 140 us -> none  [the longest x2 58.2 us: tangents(): lax.dot_general(direc, examples, (((1,), (1,)), ((), ())), preferred_elem...]
    pallas_call x7 -> x1, Pallas kernels: 118 us -> 150 us  [shards(): pl.pallas_call(functools.partial(kernel, dims), out_shape=(jax.ShapeDtype...]
    slice x6 -> x0, local copies, waits for them, and re-layouts: 4.76 us -> none  [the longest x4 3.38 us: unpack(): out.append(from_rows(x[at:at + count], like.shape))]
    convert_element_type x3 -> x0, other arithmetic: 2.99 us -> none  [the longest x2 2.27 us: reduced(): parts.append(part.astype(jnp.bfloat16))]
where the time goes in v1:
time: 156 us
  Pallas kernels  150 us (96%)
  local copies, waits for them, and re-layouts  3.64 us (2%)
    pallas_call x1, Pallas kernels, shards(): pl.pallas_call(functools.partial(kernel, dims), out_shape=(jax.ShapeDtype...  150 us

profile of v1, /device:TPU:0, one launch (start us, length us, event | category | flops | bytes accessed | tf_op | source)
XLA Modules:
  0.0 156.2 jit_solution(12883575414843709385)
XLA Ops:
  0.6 1.5 reshape.27
  2.1 150.4 %shard_map.86 = (f32[32,8192]{1,0:T(8,128)}, f32[32,8]{1,0:T(8,128)}) custom-call(bf16[1024,32768]{1,0:T(8,128)(2,1)} %x_hbm.1, f32[1,32768]{1,0:T(1,128)} %bitcast.5, s32[1,32768]{1,0:T(1,128)} %bitcast.6, s32[8,128]{1,0:T(8,128)} %bitcast.7, s32[8,128]{1,0:T(8,128)} %bitcast.8, f32[32,1024]{1,0:T(8,128)} %vw_ref.1, f32[1,256]{1,0:T(1,128)} %bitcast.9), custom_call_target="tpu_custom_call" | custom-call | tf_op jit(solution)/shard_map/pallas_call | solution.py:474
  152.6 1.4 copy.9
  153.9 2.3 %copy.11 = f32[32,8192]{1,0:T(8,128)} copy(f32[32,8192]{1,0:T(8,128)} %get-tuple-element.6) | data formatting | bytes 2097152

commit v2 on v1

--- a/solution.py
+++ b/solution.py
@@ -12,7 +12,7 @@
 VMEM = pl.BlockSpec(memory_space=pltpu.VMEM)
 ANY = pl.BlockSpec(memory_space=pl.ANY)
 LANES = 128
-LAG_SUM, LAG_LOW, LAG_TANG = 1, 3, 4
+LAG_SUM, LAG_LOW, LAG_TANG = 1, 4, 5
 RING_BYTES = 32 * 2**20
 
 
@@ -33,17 +33,14 @@
     return total
 
 
-def pick(packet, lane):
-    lanes = lax.broadcasted_iota(jnp.int32, packet.shape, 1)
-    return jnp.sum(jnp.where(lanes == lane, packet, 0.0), axis=1, keepdims=True)
-
-
-def packed(columns, rows):
+def packed(columns):
+    rows = columns[0].shape[0]
     lanes = lax.broadcasted_iota(jnp.int32, (rows, LANES), 1)
     out = jnp.zeros((rows, LANES), jnp.float32)
     for lane, column in enumerate(columns):
         out = jnp.where(lanes == lane, column, out)
-    return out
+    out = jnp.transpose(out)[:8]
+    return jnp.concatenate([out, jnp.zeros((8, LANES - rows), jnp.float32)], axis=1)
 
 
 def split_in(x, pieces):
@@ -69,15 +66,18 @@
     split_ref,
     vw_ref,
     strengths_ref,
-    solve_ref,
+    base_hbm,
+    resid_hbm,
+    coef_ref,
     hyper_ref,
     ring,
+    turned_x,
+    weights,
     margin,
     margins,
     lam,
     curvew,
     left,
-    keep,
     out_a,
     in_a,
     out_b,
@@ -86,17 +86,21 @@
     rhs,
     tang,
     parts,
+    held,
     gathered,
     sums,
-    coef,
+    alpha,
     packets,
+    feat_packets,
     grouped,
     groups,
     group_parts,
     own_groups,
     own_parts,
     own_strengths,
+    resid,
     ring_sem,
+    out_sem,
     pair_sem,
     feat_sem,
     ex_sem,
@@ -162,12 +166,17 @@
     )
     own_strengths[...] = jnp.transpose(jnp.broadcast_to(strengths_ref[...], (8, blocks)))
     margin[...] = jnp.zeros_like(margin)
+    weights[...] = w_ref[...].astype(jnp.float32)
+
+    def weight_row(start):
+        row = lax.div(start, LANES)
+        return jnp.concatenate([weights[pl.ds(row + t, 1), :] for t in range(size // LANES)], axis=1)
 
     @pl.loop(0, chunks)
     def _(i):
         arrived(i)
         slot = lax.rem(i, slots)
-        w = jnp.concatenate([columns(w_ref, i, h, x) for h in range(2) for x in range(2)], axis=1)
+        w = jnp.concatenate([weight_row((h + 2 * x) * share + i * size) for h in range(2) for x in range(2)], axis=1)
         part = lax.dot_general(
             w.astype(jnp.bfloat16), ring[slot], (((1,), (1,)), ((), ())), preferred_element_type=jnp.float32
         )
@@ -235,51 +244,68 @@
         )[kind]
         return remote(src, dst, [pair_sem.at[phase, kind, d, chunk] for d in range(2)], "ex", flip(me_e, mask))
 
-    def product(phase, finish):
+    def product(phase, finish, account):
         tang[phase] = jnp.zeros_like(tang[phase])
         base = (phase + 1) * chunks
-
-        @pl.loop(0, chunks + LAG_TANG)
-        def _(i):
-            @pl.when((i >= LAG_LOW) & (i < chunks + LAG_LOW))
-            def _():
-                chunk = i - LAG_LOW
-                pair_copy(phase, 1, chunk).wait_recv()
-                value = finish(chunk, keep[chunk] + in_b[phase, chunk].astype(jnp.float32))
-                low[phase, chunk, core] = value.astype(jnp.bfloat16)
-                pair_copy(phase, 2, chunk).start()
-
-            @pl.when((i >= LAG_SUM) & (i < chunks + LAG_SUM))
-            def _():
-                chunk = i - LAG_SUM
-                pair_copy(phase, 0, chunk).wait_recv()
-                value = keep[chunk] + in_a[phase, chunk].astype(jnp.float32)
-                keep[chunk] = value
-                out_b[phase, chunk] = value.astype(jnp.bfloat16)
-                pair_copy(phase, 1, chunk).start()
-
-            @pl.when(i < chunks)
-            def _():
+        keep = (rhs, resid)[phase]
+
+        def low_step(i):
+            chunk = i - LAG_LOW
+            pair_copy(phase, 1, chunk).wait_recv()
+            value = finish(chunk, keep[chunk] + in_b[phase, chunk].astype(jnp.float32))
+            low[phase, chunk, core] = value.astype(jnp.bfloat16)
+            pair_copy(phase, 2, chunk).start()
+
+        def sum_step(i):
+            chunk = i - LAG_SUM
+            pair_copy(phase, 0, chunk).wait_recv()
+            value = keep[chunk] + in_a[phase, chunk].astype(jnp.float32)
+            keep[chunk] = value
+            out_b[phase, chunk] = value.astype(jnp.bfloat16)
+            pair_copy(phase, 1, chunk).start()
+
+        def matmuls(i, first, second):
+            if first:
                 arrived(base + i)
                 slot = lax.rem(base + i, slots)
                 away = ring[slot, :, pl.ds(pl.multiple_of((1 - core) * half, LANES), half)]
                 out_a[phase, i] = jnp.dot(left[...], away, preferred_element_type=jnp.float32).astype(jnp.bfloat16)
                 pair_copy(phase, 0, i).start()
+            if second:
+                chunk = i - LAG_TANG
+                held_slot = lax.rem(base + chunk, slots)
+                pair_copy(phase, 2, chunk).wait_recv()
+                account(chunk)
+                turned_x[...] = jnp.transpose(ring[held_slot])
+            if first:
                 mine = ring[slot, :, pl.ds(pl.multiple_of(core * half, LANES), half)]
                 keep[i] = jnp.dot(left[...], mine, preferred_element_type=jnp.float32)
-
-            @pl.when(i >= LAG_TANG)
-            def _():
-                chunk = i - LAG_TANG
-                slot = lax.rem(base + chunk, slots)
-                pair_copy(phase, 2, chunk).wait_recv()
+            if second:
                 direc = jnp.concatenate([low[phase, chunk, 0], low[phase, chunk, 1]], axis=1)
-                part = lax.dot_general(
-                    direc, ring[slot], (((1,), (1,)), ((), ())), preferred_element_type=jnp.float32
-                )
+                part = jnp.dot(direc, turned_x[...], preferred_element_type=jnp.float32)
                 for g in range(groups_n):
                     tang[phase, g] += part[:, g * LANES : (g + 1) * LANES]
                 refill(base + chunk)
+
+        ramp = min(LAG_TANG, chunks)
+
+        @pl.loop(0, ramp)
+        def _(i):
+            pl.when((i >= LAG_LOW) & (i < chunks + LAG_LOW))(lambda: low_step(i))
+            pl.when((i >= LAG_SUM) & (i < chunks + LAG_SUM))(lambda: sum_step(i))
+            matmuls(i, True, False)
+
+        @pl.loop(ramp, chunks)
+        def _(i):
+            low_step(i)
+            sum_step(i)
+            matmuls(i, True, True)
+
+        @pl.loop(chunks, chunks + LAG_TANG)
+        def _(i):
+            pl.when((i >= LAG_LOW) & (i < chunks + LAG_LOW))(lambda: low_step(i))
+            pl.when((i >= LAG_SUM) & (i < chunks + LAG_SUM))(lambda: sum_step(i))
+            pl.when(i >= LAG_TANG)(lambda: matmuls(i, False, True))
 
     def scattered(phase):
         peers = [lax.rem(me_f + k, nf) for k in range(1, nf)]
@@ -309,17 +335,29 @@
     def own_part(ref, chunk):
         return ref[chunk, :, pl.ds(pl.multiple_of(side * size, LANES), size)]
 
+    def out_copy(phase, chunk):
+        src, dst = ((rhs, base_hbm), (resid, resid_hbm))[phase]
+        at = pl.multiple_of(side * size, LANES)
+        return pltpu.make_async_copy(
+            src.at[chunk, :, pl.ds(at, size)],
+            dst.at[:, pl.ds(pl.multiple_of(chunk * size, LANES), size)],
+            out_sem.at[phase, chunk],
+        )
+
     sums[...] = jnp.zeros_like(sums)
 
     def first_low(chunk, value):
         rhs[chunk] = value
+        return value
+
+    def first_account(chunk):
         own = own_part(rhs, chunk)
         square = own * own
         sums[0] += fold(square)
         sums[1] += fold(square * own_part(lam, chunk))
-        return value
-
-    product(0, first_low)
+        out_copy(0, chunk).start()
+
+    product(0, first_low, first_account)
 
     first_row = lax.rem(me_f, owners) * per
 
@@ -330,24 +368,24 @@
         return jnp.sum(out, axis=1, keepdims=True)
 
     mine = scattered(0)
-    gathered[me_f, 0:per] = mine
-    gathered[me_f, per] = packed(
-        [
-            jnp.sum(sums[0], axis=1, keepdims=True),
-            jnp.sum(sums[1], axis=1, keepdims=True),
-            weighted(mine, mine),
-        ],
-        rows,
+    held[...] = mine
+    for t in range(per):
+        gathered[me_f, t] = (curvew[pl.ds(first_row + t, 1), :] * mine[t]).astype(jnp.bfloat16)
+    whole_tang = launch(feat_copies(lambda peer: gathered.at[me_f], lambda k: gathered.at[me_f], 3))
+    feat_packets[0, 0] = packed(
+        [jnp.sum(sums[at], axis=1, keepdims=True) for at in range(2)] + [weighted(mine, mine)]
     )
-    receive(launch(feat_copies(lambda peer: gathered.at[me_f], lambda k: gathered.at[me_f], 3)))
-    packet = gathered[0, per]
-    for f in range(1, nf):
-        packet = packet + gathered[f, per]
+    feat_sums = launch(feat_copies(lambda peer: feat_packets.at[0, 0], lambda k: feat_packets.at[0, k], 5))
+    receive(whole_tang)
+    for g in range(groups_n):
+        left[:, g * LANES : (g + 1) * LANES] = gathered[g // per, g % per]
+    receive(feat_sums)
+    packet = feat_packets[0, 0]
+    for k in range(1, nf):
+        packet = packet + feat_packets[0, k]
     packets[0, 0] = packet
     shared = launch(ex_copies(lambda peer: packets.at[0, 0], lambda k: packets.at[0, k], 0))
     waiting.extend(shared)
-    for g in range(groups_n):
-        left[:, g * LANES : (g + 1) * LANES] = (curvew[g : g + 1] * gathered[g // per, g % per]).astype(jnp.bfloat16)
 
     sums[...] = jnp.zeros_like(sums)
     grouped[...] = jnp.zeros_like(grouped)
@@ -360,23 +398,25 @@
             packet = packets[0, 0]
             for k in range(1, ne):
                 packet = packet + packets[0, k]
-            norm, damp, along = (pick(packet, lane) for lane in range(3))
-            alpha = norm / (along / total + damp)
-            for at, column in enumerate((alpha, norm, damp, along)):
-                coef[at] = jnp.broadcast_to(column, (rows, LANES))
+            norm, damp, along = packet[0:1], packet[1:2], packet[2:3]
+            steps = norm / (along / total + damp)
+            packets[3, 0] = jnp.concatenate([steps, packet[:7]], axis=0)
+            alpha[...] = jnp.transpose(packets[3, 0])[:rows, 0:1]
 
         base = rhs[chunk]
-        value = base - coef[0, :, 0:1] * (value / total + lam[chunk] * base)
-        keep[chunk] = value
-        own = own_part(keep, chunk)
+        value = base - alpha[...] * (value / total + lam[chunk] * base)
+        resid[chunk] = value
+        return value
+
+    def second_account(chunk):
+        own = own_part(resid, chunk)
         before = own_part(rhs, chunk)
         scaled = own_part(lam, chunk) * own
         sums[0] += fold(own * own)
         sums[1] += fold(scaled * own)
         sums[2] += fold(scaled * before)
-        solve_ref[:, pl.ds(pl.multiple_of(chunk * size, LANES), size)] = own
         at = pl.multiple_of(me_e * share + chunk * size, LANES)
-        w = w_ref[:, pl.ds(at, size)]
+        w = weight_row(at)
         pieces = jnp.concatenate(split_in(before * w, 2) + split_in(own * w, 2), axis=0)
         grouped[...] += lax.dot_general(
             one_hot(ids_ref[:, pl.ds(at, size)], blocks),
@@ -384,62 +424,54 @@
             (((1,), (1,)), ((), ())),
             preferred_element_type=jnp.float32,
         )
-        return value
-
-    product(1, second_low)
+        out_copy(1, chunk).start()
+
+    product(1, second_low, second_account)
 
     for f in range(nf):
         groups[f] = grouped[f * nb_feat : (f + 1) * nb_feat, :]
     sent = launch(feat_copies(lambda peer: groups.at[peer], lambda k: group_parts.at[k], 4))
     turned = scattered(1)
+    packets[1, 0] = packed(
+        [jnp.sum(sums[at], axis=1, keepdims=True) for at in range(3)]
+        + [weighted(turned, turned), weighted(turned, held[...])]
+    )
+    ex_sums = launch(ex_copies(lambda peer: packets.at[1, 0], lambda k: packets.at[1, k], 1))
     receive(sent)
     owned = groups[me_f]
     for k in range(1, nf):
         owned = owned + group_parts[k]
     for e in range(ne):
         own_groups[e] = owned[e * nb_own : (e + 1) * nb_own, :]
-    held = gathered[me_f, 0:per]
-    packets[1, 0] = packed(
-        [jnp.sum(sums[at], axis=1, keepdims=True) for at in range(3)]
-        + [weighted(turned, turned), weighted(turned, held)],
-        rows,
-    )
-    receive(
-        launch(
-            ex_copies(lambda peer: packets.at[1, 0], lambda k: packets.at[1, k], 1)
-            + ex_copies(lambda peer: own_groups.at[peer], lambda k: own_parts.at[k], 2)
-        )
-    )
+    group_sums = launch(ex_copies(lambda peer: own_groups.at[peer], lambda k: own_parts.at[k], 2))
+    receive(ex_sums)
     packet = packets[1, 0]
     for k in range(1, ne):
         packet = packet + packets[1, k]
-    packets[2, 0] = packet
-    receive(launch(feat_copies(lambda peer: packets.at[2, 0], lambda k: parts.at[2, k, 0], 5)))
+    feat_packets[1, 0] = packet
+    feat_sums = launch(feat_copies(lambda peer: feat_packets.at[1, 0], lambda k: feat_packets.at[1, k], 6))
+    receive(group_sums)
+    mine = own_groups[me_e]
+    for k in range(1, ne):
+        mine = mine + own_parts[k]
+    first_block = (me_f * ne + me_e) * nb_own
+    mine = -own_strengths[pl.ds(first_block, nb_own), 0:1] * mine
+    receive(feat_sums)
     for k in range(1, nf):
-        packet = packet + parts[2, k, 0]
-
-    norm_next, damp_next, damp_cross, curved_next, curved_cross = (pick(packet, lane) for lane in range(5))
-    alpha, norm, damp, along = (coef[at, :, 0:1] for at in range(4))
+        packet = packet + feat_packets[1, k]
+
+    norm_next, damp_next, damp_cross, curved_next, curved_cross = (packet[at : at + 1, :rows] for at in range(5))
+    before = packets[3, 0]
+    alphas, norm, damp, along = (before[at : at + 1, :rows] for at in range(4))
     beta = norm_next / norm
     curved = curved_next + 2.0 * beta * curved_cross + beta * beta * along
     damped = damp_next + 2.0 * beta * damp_cross + beta * beta * damp
     step = norm_next / (curved / total + damped)
-    first = alpha + step * beta
-
-    @pl.loop(0, chunks)
-    def _(i):
-        at = pl.ds(pl.multiple_of(i * size, LANES), size)
-        solve_ref[:, at] = first * own_part(rhs, i) + step * solve_ref[:, at]
-
-    mine = own_groups[me_e]
-    for k in range(1, ne):
-        mine = mine + own_parts[k]
-    first_block = (me_f * ne + me_e) * nb_own
-    scale = own_strengths[pl.ds(first_block, nb_own), 0:1]
-    mine = jnp.concatenate([-scale * mine, jnp.zeros((8 * pl.cdiv(nb_own, 8) - nb_own, LANES), jnp.float32)], axis=0) if nb_own % 8 else -scale * mine
-    mine = jnp.transpose(mine)[:, :nb_own]
-    hyper_ref[...] = first * (mine[:rows] + mine[rows : 2 * rows]) + step * (
-        mine[2 * rows : 3 * rows] + mine[3 * rows : 4 * rows]
+    first = alphas + step * beta
+    coef_ref[0:1, :rows] = first
+    coef_ref[1:2, :rows] = step
+    hyper_ref[...] = first * (mine[:, :rows] + mine[:, rows : 2 * rows]) + step * (
+        mine[:, 2 * rows : 3 * rows] + mine[:, 3 * rows : 4 * rows]
     )
 
     for copy in waiting:
@@ -448,6 +480,7 @@
     @pl.loop(0, chunks)
     def _(i):
         for phase in range(2):
+            out_copy(phase, i).wait()
             for kind in range(3):
                 pair_copy(phase, kind, i).wait_send()
 
@@ -471,22 +504,25 @@
     dims = (nf, ne, n, width, rows, blocks, share, size, chunks, slots)
     half = 2 * size
     f32, bf16 = jnp.float32, jnp.bfloat16
-    return pl.pallas_call(
+    base, resid, coef, hyper = pl.pallas_call(
         functools.partial(kernel, dims),
         out_shape=(
             jax.ShapeDtypeStruct((rows, share), f32),
-            jax.ShapeDtypeStruct((rows, nb_own), f32),
+            jax.ShapeDtypeStruct((rows, share), f32),
+            jax.ShapeDtypeStruct((8, LANES), f32),
+            jax.ShapeDtypeStruct((nb_own, rows), f32),
         ),
         in_specs=[ANY] + [VMEM] * 6,
-        out_specs=(VMEM, VMEM),
+        out_specs=(ANY, ANY, VMEM, VMEM),
         scratch_shapes=[
             pltpu.VMEM((slots, n, 2 * half), bf16),
+            pltpu.VMEM((2 * half, n), bf16),
+            pltpu.VMEM((width // LANES, LANES), f32),
             pltpu.VMEM((groups_n, LANES), f32),
             pltpu.VMEM((nf, groups_n, LANES), f32),
             pltpu.VMEM((chunks, 1, half), f32),
             pltpu.VMEM((groups_n, LANES), f32),
             pltpu.VMEM((rows, n), bf16),
-            pltpu.VMEM((chunks, rows, half), f32),
             pltpu.VMEM((2, chunks, rows, half), bf16),
             pltpu.VMEM((2, chunks, rows, half), bf16),
             pltpu.VMEM((2, chunks, rows, half), bf16),
@@ -494,20 +530,24 @@
             pltpu.VMEM((2, chunks, 2, rows, half), bf16),
             pltpu.VMEM((chunks, rows, half), f32),
             pltpu.VMEM((2, groups_n, rows, LANES), f32),
-            pltpu.VMEM((3, nf, per, rows, LANES), f32),
-            pltpu.VMEM((nf, per + 1, rows, LANES), f32),
+            pltpu.VMEM((2, nf, per, rows, LANES), f32),
+            pltpu.VMEM((per, rows, LANES), f32),
+            pltpu.VMEM((nf, per, rows, LANES), bf16),
             pltpu.VMEM((3, rows, LANES), f32),
-            pltpu.VMEM((4, rows, LANES), f32),
-            pltpu.VMEM((3, ne, rows, LANES), f32),
+            pltpu.VMEM((rows, 1), f32),
+            pltpu.VMEM((4, ne, 8, LANES), f32),
+            pltpu.VMEM((2, nf, 8, LANES), f32),
             pltpu.VMEM((blocks, 4 * rows), f32),
             pltpu.VMEM((nf, nb_feat, 4 * rows), f32),
             pltpu.VMEM((nf, nb_feat, 4 * rows), f32),
             pltpu.VMEM((ne, nb_own, 4 * rows), f32),
             pltpu.VMEM((ne, nb_own, 4 * rows), f32),
             pltpu.VMEM((blocks, 8), f32),
+            pltpu.VMEM((chunks, rows, half), f32),
             pltpu.SemaphoreType.DMA((slots, 4)),
+            pltpu.SemaphoreType.DMA((2, chunks)),
             pltpu.SemaphoreType.DMA((2, 3, 2, chunks)),
-            pltpu.SemaphoreType.DMA((6, 2, nf)),
+            pltpu.SemaphoreType.DMA((7, 2, nf)),
             pltpu.SemaphoreType.DMA((3, 2, ne)),
         ],
         compiler_params=pltpu.CompilerParams(
@@ -515,13 +555,15 @@
         ),
     )(
         examples,
-        weights.astype(f32).reshape(1, width),
+        weights.reshape(width // LANES, LANES),
         block_ids.reshape(1, width),
         labels.reshape(groups_n, LANES),
         split.reshape(groups_n, LANES),
         val_weight,
         strengths.reshape(1, blocks),
     )
+    solve = coef[0, :rows, None] * base + coef[1, :rows, None] * resid
+    return (solve, hyper.T)
 
 
 def solution(mesh):

time: 156 us -> 138 us (0.88)
  Pallas kernels: 150 us -> 133 us
  local copies, waits for them, and re-layouts: 3.64 us -> 2.03 us
    pallas_call x1, Pallas kernels: 150 us -> 133 us  [shards(): pl.pallas_call(functools.partial(kernel, dims), out_shape=(jax.ShapeDtype...]
    add x0 -> x1, other arithmetic: none -> 2.69 us  [shards(): solve = coef[0, :rows, None] * base + coef[1, :rows, None] * resid]
where the time goes in v2:
time: 138 us
  Pallas kernels  133 us (96%)
  other arithmetic  2.69 us (2%)
  local copies, waits for them, and re-layouts  2.03 us (1%)
    pallas_call x1, Pallas kernels, shards(): pl.pallas_call(functools.partial(kernel, dims), out_shape=(jax.ShapeDtype...  133 us

profile of v2, /device:TPU:0, one launch (start us, length us, event | category | flops | bytes accessed | tf_op | source)
XLA Modules:
  0.0 137.9 jit_solution(8306530280136618479)
XLA Ops:
  0.6 132.6 %shard_map.86 = (f32[32,8192]{1,0:T(8,128)}, f32[32,8192]{1,0:T(8,128)}, f32[8,128]{1,0:T(8,128)}, f32[8,32]{1,0:T(8,128)}) custom-call(bf16[1024,32768]{1,0:T(8,128)(2,1)} %x_hbm.1, bf16[256,128]{1,0:T(8,128)(2,1)} %bitcast.11, s32[1,32768]{1,0:T(1,128)} %bitcast.10, s32[8,128]{1,0:T(8,128)} %bitcast.12, s32[8,128]{1,0:T(8,128)} %bitcast.13, ...), custom_call_target="tpu_custom_call" | custom-call | tf_op jit(solution)/shard_map/pallas_call | solution.py:507
  133.2 0.8 slice_bitcast_fusion.1
  134.0 2.7 %multiply_add_fusion = f32[32,8192]{1,0:T(8,128)} fusion(f32[32,8192]{1,0:T(8,128)} %get-tuple-element.8, f32[32,8192]{1,0:T(8,128)} %get-tuple-element.7, f32[32]{0:T(128)S(1)} %get-tuple-element.11, f32[32]{0:T(128)S(1)} %get-tuple-element.10), kind=kLoop, calls=%fused_computation | loop fusion | flops 786432 | bytes 3145984 | tf_op jit(solution)/shard_map/add | solution.py:565
  136.7 1.3 copy.10

commit v3 on v2

--- a/solution.py
+++ b/solution.py
@@ -218,6 +218,10 @@
 
     waiting = []
 
+    def settle():
+        while waiting:
+            waiting.pop().wait_send()
+
     def receive(copies):
         for copy in copies:
             copy.wait_recv()
@@ -276,13 +280,25 @@
                 held_slot = lax.rem(base + chunk, slots)
                 pair_copy(phase, 2, chunk).wait_recv()
                 account(chunk)
-                turned_x[...] = jnp.transpose(ring[held_slot])
+                if first:
+                    turned_x[...] = jnp.transpose(ring[held_slot])
+                else:
+                    turned_x[:half] = jnp.transpose(ring[held_slot, :, :half])
             if first:
                 mine = ring[slot, :, pl.ds(pl.multiple_of(core * half, LANES), half)]
                 keep[i] = jnp.dot(left[...], mine, preferred_element_type=jnp.float32)
-            if second:
+            if second and first:
                 direc = jnp.concatenate([low[phase, chunk, 0], low[phase, chunk, 1]], axis=1)
                 part = jnp.dot(direc, turned_x[...], preferred_element_type=jnp.float32)
+            elif second:
+                part = jnp.dot(low[phase, chunk, 0], turned_x[:half], preferred_element_type=jnp.float32)
+                part = part + lax.dot_general(
+                    low[phase, chunk, 1],
+                    ring[held_slot, :, half:],
+                    (((1,), (1,)), ((), ())),
+                    preferred_element_type=jnp.float32,
+                )
+            if second:
                 for g in range(groups_n):
                     tang[phase, g] += part[:, g * LANES : (g + 1) * LANES]
                 refill(base + chunk)
@@ -307,16 +323,28 @@
             pl.when((i >= LAG_SUM) & (i < chunks + LAG_SUM))(lambda: sum_step(i))
             pl.when(i >= LAG_TANG)(lambda: matmuls(i, False, True))
 
-    def scattered(phase):
+    def settle_product(phase):
+        @pl.loop(0, chunks)
+        def _(i):
+            out_copy(phase, i).wait()
+            for kind in range(3):
+                pair_copy(phase, kind, i).wait_send()
+
+    def scattered(phase, meanwhile):
         peers = [lax.rem(me_f + k, nf) for k in range(1, nf)]
         copies = feat_copies(
             lambda peer: tang.at[phase, pl.ds(lax.rem(peer, owners) * per, per)], lambda k: parts.at[phase, k], 1 + phase
         )
         if owners == nf:
-            receive(launch(copies))
+            launch(copies)
+            sent = meanwhile()
+            settle()
+            receive(copies)
         else:
             for peer, copy in zip(peers, copies):
                 pl.when(peer < owners)(copy.start)
+            sent = meanwhile()
+            settle()
 
             @pl.when(me_f < owners)
             def _():
@@ -329,8 +357,8 @@
         for k in range(1, nf):
             value = value + parts[phase, k]
         if owners == nf:
-            return value
-        return jnp.where(me_f < owners, value, 0.0)
+            return value, sent
+        return jnp.where(me_f < owners, value, 0.0), sent
 
     def own_part(ref, chunk):
         return ref[chunk, :, pl.ds(pl.multiple_of(side * size, LANES), size)]
@@ -367,7 +395,7 @@
             out = out + curvew[pl.ds(first_row + t, 1), :] * value[t] * other[t]
         return jnp.sum(out, axis=1, keepdims=True)
 
-    mine = scattered(0)
+    mine, _ = scattered(0, lambda: settle_product(0))
     held[...] = mine
     for t in range(per):
         gathered[me_f, t] = (curvew[pl.ds(first_row + t, 1), :] * mine[t]).astype(jnp.bfloat16)
@@ -428,10 +456,14 @@
 
     product(1, second_low, second_account)
 
-    for f in range(nf):
-        groups[f] = grouped[f * nb_feat : (f + 1) * nb_feat, :]
-    sent = launch(feat_copies(lambda peer: groups.at[peer], lambda k: group_parts.at[k], 4))
-    turned = scattered(1)
+    def send_groups():
+        for f in range(nf):
+            groups[f] = grouped[f * nb_feat : (f + 1) * nb_feat, :]
+        sent = launch(feat_copies(lambda peer: groups.at[peer], lambda k: group_parts.at[k], 4))
+        settle_product(1)
+        return sent
+
+    turned, sent = scattered(1, send_groups)
     packets[1, 0] = packed(
         [jnp.sum(sums[at], axis=1, keepdims=True) for at in range(3)]
         + [weighted(turned, turned), weighted(turned, held[...])]
@@ -456,6 +488,7 @@
         mine = mine + own_parts[k]
     first_block = (me_f * ne + me_e) * nb_own
     mine = -own_strengths[pl.ds(first_block, nb_own), 0:1] * mine
+    settle()
     receive(feat_sums)
     for k in range(1, nf):
         packet = packet + feat_packets[1, k]
@@ -468,21 +501,20 @@
     damped = damp_next + 2.0 * beta * damp_cross + beta * beta * damp
     step = norm_next / (curved / total + damped)
     first = alphas + step * beta
-    coef_ref[0:1, :rows] = first
-    coef_ref[1:2, :rows] = step
+    coef_ref[...] = jnp.concatenate(
+        [jnp.broadcast_to(x, (4, rows)) for x in (first, step)], axis=0
+    )
     hyper_ref[...] = first * (mine[:, :rows] + mine[:, rows : 2 * rows]) + step * (
         mine[:, 2 * rows : 3 * rows] + mine[:, 3 * rows : 4 * rows]
     )
 
-    for copy in waiting:
-        copy.wait_send()
-
-    @pl.loop(0, chunks)
-    def _(i):
-        for phase in range(2):
-            out_copy(phase, i).wait()
-            for kind in range(3):
-                pair_copy(phase, kind, i).wait_send()
+    settle()
+
+
+def combine(base_ref, resid_ref, coef_ref, blocks_ref, solve_ref, hyper_ref):
+    columns = jnp.transpose(coef_ref[...])
+    solve_ref[...] = columns[:, 0:1] * base_ref[...] + columns[:, 4:5] * resid_ref[...]
+    hyper_ref[...] = blocks_ref[...]
 
 
 def shards(examples, weights, labels, split, val_weight, strengths, block_ids):
@@ -509,7 +541,7 @@
         out_shape=(
             jax.ShapeDtypeStruct((rows, share), f32),
             jax.ShapeDtypeStruct((rows, share), f32),
-            jax.ShapeDtypeStruct((8, LANES), f32),
+            jax.ShapeDtypeStruct((8, rows), f32),
             jax.ShapeDtypeStruct((nb_own, rows), f32),
         ),
         in_specs=[ANY] + [VMEM] * 6,
@@ -562,7 +594,15 @@
         val_weight,
         strengths.reshape(1, blocks),
     )
-    solve = coef[0, :rows, None] * base + coef[1, :rows, None] * resid
+    block = pl.BlockSpec((rows, share // 4), lambda i: (0, i))
+    same = lambda like: pl.BlockSpec(like.shape, lambda i: (0, 0))
+    solve, hyper = pl.pallas_call(
+        combine,
+        grid=(4,),
+        out_shape=(jax.ShapeDtypeStruct(base.shape, f32), jax.ShapeDtypeStruct(hyper.shape, f32)),
+        in_specs=[block, block, same(coef), same(hyper)],
+        out_specs=(block, same(hyper)),
+    )(base, resid, coef, hyper)
     return (solve, hyper.T)
 
 

time: 138 us -> 133 us (0.964)
  other arithmetic: 2.69 us -> 0 us
  local copies, waits for them, and re-layouts: 2.03 us -> 0 us
    pallas_call x1, Pallas kernels: 133 us -> 128 us  [shards(): pl.pallas_call(functools.partial(kernel, dims), out_shape=(jax.ShapeDtype...]
    pallas_call x0 -> x1, Pallas kernels: none -> 3.86 us  [shards(): pl.pallas_call(combine, grid=(4,), out_shape=(jax.ShapeDtypeStruct(base.s...]
    add x1 -> x0, other arithmetic: 2.69 us -> none  [shards(): solve = coef[0, :rows, None] * base + coef[1, :rows, None] * resid]
where the time goes in v3:
time: 133 us; the launch traced here: 132 us
  Pallas kernels  132 us (99%)
    pallas_call x1, Pallas kernels, shards(): pl.pallas_call(functools.partial(kernel, dims), out_shape=(jax.ShapeDtype...  128 us
    pallas_call x1, Pallas kernels, shards(): pl.pallas_call(combine, grid=(4,), out_shape=(jax.ShapeDtypeStruct(base.s...  3.86 us

profile of v3, /device:TPU:0, one launch (start us, length us, event | category | flops | bytes accessed | tf_op | source)
XLA Modules:
  0.0 132.5 jit_solution(7625741387062228948)
XLA Ops:
  0.6 128.0 %shard_map.86 = (f32[32,8192]{1,0:T(8,128)}, f32[32,8192]{1,0:T(8,128)}, f32[8,32]{1,0:T(8,128)}, f32[8,32]{1,0:T(8,128)}) custom-call(bf16[1024,32768]{1,0:T(8,128)(2,1)} %x_hbm.1, bf16[256,128]{1,0:T(8,128)(2,1)} %bitcast.7, s32[1,32768]{1,0:T(1,128)} %bitcast.6, s32[8,128]{1,0:T(8,128)} %bitcast.8, s32[8,128]{1,0:T(8,128)} %bitcast.9, f32[32,1024]{1,0:T(8,128)} %vw_ref.1, ...), custom_call_target="tpu_custom_call" | custom-call | tf_op jit(solution)/shard_map/pallas_call | solution.py:539
  128.6 3.9 %shard_map.87 = (f32[32,8192]{1,0:T(8,128)}, f32[8,32]{1,0:T(8,128)}) custom-call(f32[32,8192]{1,0:T(8,128)} %get-tuple-element.8.base_ref, f32[32,8192]{1,0:T(8,128)} %get-tuple-element.9.resid_ref, f32[8,32]{1,0:T(8,128)} %get-tuple-element.10.coef_ref, f32[8,32]{1,0:T(8,128)} %get-tuple-element.11.blocks_ref), custom_call_target="tpu_custom_call" | custom-call | tf_op jit(solution)/shard_map/pallas_call | solution.py:599
